TPU v7x, 256 devices: a whole 4x4x8 slice. The times are simulated.
256 devices in a mesh: row: 8 (over x, core), col: 32 (over y, z).
Axes of the slice: x: 4, y: 4, z: 8, core: 2. Of those that a mesh axis runs over, the one named last changes fastest.
Arguments:
- hidden: bfloat16 [4096, 8192], P('row', 'col'), may hold values from -600 to 600
- norm_gain: float32 [8192], replicated, may hold values from 0.5 to 2
- wq: bfloat16 [8192, 8192], P('row', 'col'), may hold values from -1 to 1
- wk: bfloat16 [8192, 1024], P('row', 'col'), may hold values from -1 to 1
- wv: bfloat16 [8192, 1024], P('row', 'col'), may hold values from -0.0625 to 0.0625
- wo: bfloat16 [8192, 8192], P('row', 'col'), may hold values from -0.25 to 0.25
Outputs:
- attn_out: bfloat16 [4096, 8192], P('row', 'col')
All inputs are finite; a program needn't handle non-finite values.
Results may differ from a plain program's by a relative error of at most 0.011.
Values may be sent and summed in bfloat16 or wider, within the bound.
A program may use at most 64 MiB of HBM per device.

v0:
```python
import jax
import jax.numpy as jnp
from jax import lax
from jax.sharding import PartitionSpec as P

HD = 128


def partner(array, axis, distance):
    return lax.ppermute(array, axis, [(i, i ^ 1 << distance) for i in range(lax.axis_size(axis))])


def rotary(field, positions):
    half = field.shape[-1] // 2
    steps = jnp.arange(half).astype(jnp.float32)
    freqs = 10000.0 ** (-steps / half)
    angles = positions.astype(jnp.float32)[:, None] * freqs[None, :]
    cosine = jnp.cos(angles)[:, None, :]
    sine = jnp.sin(angles)[:, None, :]
    first = field[..., :half]
    second = field[..., half:]
    return jnp.concatenate(
        [first * cosine - second * sine, second * cosine + first * sine], axis=-1
    )


def order_pair(mine, other, col_index, bit, axis_dim):
    upper = col_index // 2**bit % 2 == 1
    lower_part = jnp.where(upper, other, mine)
    upper_part = jnp.where(upper, mine, other)
    return jnp.concatenate([lower_part, upper_part], axis=axis_dim)


def per_device(hidden, norm_gain, wq, wk, wv, wo):
    tok_rows = hidden.shape[0]
    panel = lax.all_gather(hidden, "col", axis=1, tiled=True)
    values_in = panel.astype(jnp.float32)
    meansq = jnp.mean(values_in * values_in, axis=1, keepdims=True)
    normed = (values_in * lax.rsqrt(meansq + 1e-05) * norm_gain).astype(jnp.bfloat16)
    kv_cols = wk.shape[1]
    group = max(1, HD // kv_cols)
    bits = group.bit_length() - 1
    col_index = lax.axis_index("col")
    stacked = jnp.stack((wk, wv), axis=1)
    for bit in range(bits):
        other = partner(stacked, "col", bit)
        stacked = order_pair(stacked, other, col_index, bit, 2)
    columns = normed
    query_part = jnp.dot(
        columns, lax.all_gather(wq, "row", axis=0, tiled=True), preferred_element_type=jnp.float32
    )
    pair_part = jnp.einsum(
        "ho,omr->hmr",
        columns,
        lax.all_gather(stacked, "row", axis=0, tiled=True),
        preferred_element_type=jnp.float32,
    )
    heads_here = wq.shape[1] // HD
    kv_here = pair_part.shape[2] // HD
    per_kv = heads_here // kv_here
    positions = lax.axis_index("row") * tok_rows + jnp.arange(tok_rows)
    queries = rotary(query_part.reshape(tok_rows, heads_here, HD), positions).astype(jnp.bfloat16)
    queries = queries.reshape(tok_rows, kv_here, per_kv, HD)
    keys = rotary(pair_part[:, 0].reshape(tok_rows, kv_here, HD), positions).astype(jnp.bfloat16)
    values = pair_part[:, 1].reshape(tok_rows, kv_here, HD).astype(jnp.bfloat16)
    scale = HD ** (-0.5)
    best = jnp.full((kv_here, per_kv, tok_rows), -1e30, jnp.float32)
    key_piece = lax.all_gather(keys, "row", axis=0, tiled=True)
    value_piece = lax.all_gather(values, "row", axis=0, tiled=True)
    count = key_piece.shape[0]
    scores = (
        jnp.einsum("tagd,nad->agtn", queries, key_piece, preferred_element_type=jnp.float32) * scale
    )
    key_pos = jnp.arange(count)
    visible = positions[:, None] >= key_pos[None, :]
    scores = jnp.where(visible, scores, -jnp.inf)
    fresh = jnp.maximum(best, jnp.max(scores, axis=3))
    probs = jnp.exp(scores - fresh[..., None])
    total = jnp.sum(probs, axis=3)
    update = jnp.einsum(
        "agtn,nad->agtd",
        probs.astype(jnp.bfloat16),
        value_piece,
        preferred_element_type=jnp.float32,
    )
    numer = update
    best, total, numer = (fresh, total, numer)
    heads = (
        (numer / total[..., None])
        .transpose(2, 0, 1, 3)
        .reshape(tok_rows, heads_here * HD)
        .astype(jnp.bfloat16)
    )
    head_panel = lax.all_gather(heads, "col", axis=1, tiled=True)
    columns = head_panel
    result = jnp.dot(
        columns, lax.all_gather(wo, "row", axis=0, tiled=True), preferred_element_type=jnp.float32
    )
    return result.astype(jnp.bfloat16)


def solution(mesh):
    in_specs = (
        P("row", "col"),
        P(),
        P("row", "col"),
        P("row", "col"),
        P("row", "col"),
        P("row", "col"),
    )
    out_specs = P("row", "col")
    return jax.shard_map(
        per_device, mesh=mesh, in_specs=in_specs, out_specs=out_specs, check_vma=False
    )
```

profile of v0, /device:TPU:5, one launch (start us, length us, event | category | flops | bytes accessed | tf_op | source)
XLA Modules:
  0.0 396.0 jit_solution(9538606364416327431)
XLA Ops:
  6.5 0.7 all-gather.8.cloned.1.call-update
  7.3 0.9 pad_maximum_fusion.2
  8.2 1.7 collective-permute-start
  9.9 3.1 collective-permute-done
  13.0 0.9 broadcast_select_fusion.3
  13.9 3.1 collective-permute-start.1
  17.0 11.3 %collective-permute-done.1 = bf16[1024,2,64]{0,2,1:T(8,128)(2,1)S(1)} collective-permute-done((bf16[1024,2,64]{0,2,1:T(8,128)(2,1)S(1)}, bf16[1024,2,64]{0,2,1:T(8,128)(2,1)S(1)}, u32[]{:S(2)}, u32[]{:S(2)}) %collective-permute-start.1) | collective-permute-done | bytes 262176 | tf_op jit(solution)/shard_map/ppermute | solution.py:10
  28.5 0.8 pad_maximum_fusion
  29.4 0.7 all-gather.14.cloned.1.call-update
  30.2 86.1 %all-gather.8.cloned.1.call-done = bf16[512,8192]{1,0:T(8,128)(2,1)} async-done(((bf16[512,256]{1,0:T(8,128)(2,1)}), bf16[512,8192]{1,0:T(8,128)(2,1)}) %all-gather.8.cloned.1.call-update) | async-done | bytes 8388624 | tf_op jit(solution)/shard_map/all_gather | solution.py:36
  116.3 5.1 %fusion = f32[512]{0:T(512)S(1)} fusion(bf16[512,8192]{1,0:T(8,128)(2,1)} %all-gather.8.cloned.1.call-done), kind=kLoop, calls=%fused_computation.2 | loop fusion | flops 12582400 | bytes 8390656 | tf_op jit(solution)/shard_map/reduce_sum | solution.py:38
  121.4 30.5 %all-gather.10.cloned.1.call-done = bf16[8192,2,128]{0,2,1:T(8,128)(2,1)} async-done(((bf16[1024,2,128]{0,2,1:T(8,128)(2,1)}), bf16[8192,2,128]{0,2,1:T(8,128)(2,1)}) %all-gather.10.cloned.1.call-update) | async-done | bytes 4194320 | tf_op jit(solution)/shard_map/all_gather | solution.py:55
  151.9 7.0 %fusion.12 = f32[512,256]{0,1:S(1)} fusion(bf16[8192,256]{0,1:T(8,128)(2,1)} %bitcast.61, bf16[512,8192]{1,0:T(8,128)(2,1)} %all-gather.8.cloned.1.call-done, f32[8192]{0:T(1024)S(1)} %copy-done.1, f32[512]{0:T(512)S(1)} %add_rsqrt_fusion), kind=kOutput, calls=%fused_computation.15 | convolution fusion | flops 2164260864 | bytes 13142016
  158.9 0.6 fusion.35
  159.5 0.7 pad_maximum_fusion.3
  160.2 0.7 slice.34
  161.0 0.5 all-gather.20.cloned.1.call-update
  161.5 0.2 all-gather.18.cloned.1.call-start
  161.8 1.8 multiply_cosine_fusion
  163.6 1.7 iota_compare_fusion
  165.3 23.2 %all-gather.14.cloned.1.call-done = bf16[8192,256]{1,0:T(8,128)(2,1)} async-done(((bf16[1024,256]{1,0:T(8,128)(2,1)}), bf16[8192,256]{1,0:T(8,128)(2,1)}) %all-gather.14.cloned.1.call-update) | async-done | bytes 4194320 | tf_op jit(solution)/shard_map/all_gather | solution.py:50
  188.4 7.6 %fusion.10 = f32[512,256]{0,1:T(8,128)S(1)} fusion(bf16[8192,256]{1,0:T(8,128)(2,1)} %all-gather.14.cloned.1.call-done, bf16[512,8192]{1,0:T(8,128)(2,1)} %all-gather.8.cloned.1.call-done, f32[8192]{0:T(1024)S(1)} %copy-done.1, f32[512]{0:T(512)S(1)} %add_rsqrt_fusion), kind=kOutput, calls=%fused_computation.14 | convolution fusion | flops 2164260864 | bytes 13142016 | tf_op jit(solution)/shard_map/dot_general | solution.py:49
  196.5 1.9 subtract_convert_fusion
  198.4 17.6 %all-gather.12.cloned.1.call-done = bf16[4096,1,128]{0,2,1:T(8,128)(2,1)} async-done(((bf16[512,1,128]{0,2,1:T(8,128)(2,1)}), bf16[4096,1,128]{0,2,1:T(8,128)(2,1)}) %all-gather.12.cloned.1.call-update) | async-done | bytes 1048592 | tf_op jit(solution)/shard_map/all_gather | solution.py:68
  216.0 5.1 %fusion.5 = (f32[2,512]{1,0:T(2,128)S(1)}, f32[4096,512,2]{1,0,2:T(8,128)S(1)}) fusion(pred[512,4096]{0,1:T(8,128)(4,1)S(1)} %iota_compare_fusion, bf16[512,2,64]{2,0,1:T(8,128)(2,1)} %get-tuple-element.6, bf16[512,2,64]{2,0,1:T(8,128)(2,1)S(1)} %get-tuple-element.5, bf16[4096,1,128]{0,2,1:T(8,128)(2,1)} %all-gather.12.cloned.1.call-done), kind=kOutput, calls=%fused_computation.9 | convolution fusion | flops 1086848000 | bytes 20189184 | tf_op jit(solution)/shard_map/tagd,nad->agtn/dot_general | solution.py:72
  221.0 5.7 %copy-done = f32[4096,512,2]{1,0,2:T(8,128)} copy-done((f32[4096,512,2]{1,0,2:T(8,128)}, f32[4096,512,2]{1,0,2:T(8,128)S(1)}, u32[]{:S(2)}) %copy-start) | copy-done | bytes 16777240
  226.7 4.2 %fusion.3 = f32[2,512]{1,0:T(2,128)S(1)} fusion(f32[4096,512,2]{1,0,2:T(8,128)S(1)} %get-tuple-element.18, f32[2,512]{1,0:T(2,128)S(1)} %broadcast_maximum_fusion, pred[512,4096]{0,1:T(8,128)(4,1)S(1)} %iota_compare_fusion), kind=kLoop, calls=%fused_computation.7 | loop fusion | flops 16776192 | bytes 18882560 | tf_op jit(solution)/shard_map/reduce_sum | solution.py:79
  230.9 12.6 %all-gather.16.cloned.1.call-done = bf16[4096,1,128]{0,2,1:T(8,128)(2,1)} async-done(((bf16[512,1,128]{0,2,1:T(8,128)(2,1)}), bf16[4096,1,128]{0,2,1:T(8,128)(2,1)}) %all-gather.16.cloned.1.call-update) | async-done | bytes 1048592 | tf_op jit(solution)/shard_map/all_gather | solution.py:69
  243.5 11.7 %fusion.22 = bf16[2,512,128]{1,2,0:T(8,128)(2,1)} fusion(f32[4096,512,2]{1,0,2:T(8,128)} %copy-done, f32[2,512]{1,0:T(2,128)S(1)} %broadcast_maximum_fusion, pred[512,4096]{0,1:T(8,128)(4,1)S(1)} %iota_compare_fusion, bf16[4096,1,128]{0,2,1:T(8,128)(2,1)} %all-gather.16.cloned.1.call-done, f32[2,512]{1,0:T(2,128)S(1)} %fusion.3), kind=kOutput, calls=%fused_computation.21 | convolution fusion | flops 1090781184 | bytes 20193280 | tf_op jit(solution)/shard_map/agtn,nad->agtd/dot_general | solution.py:80
  255.2 24.7 %all-gather.20.cloned.1.call-done = bf16[8192,256]{1,0:T(8,128)(2,1)} async-done(((bf16[1024,256]{1,0:T(8,128)(2,1)}), bf16[8192,256]{1,0:T(8,128)(2,1)}) %all-gather.20.cloned.1.call-update) | async-done | bytes 4194320 | tf_op jit(solution)/shard_map/all_gather | solution.py:97
  279.9 101.6 %all-gather.18.cloned.1.call-done = bf16[512,8192]{0,1:T(8,128)(2,1)} async-done(((bf16[512,256]{0,1:T(8,128)(2,1)}), bf16[512,8192]{0,1:T(8,128)(2,1)}) %all-gather.18.cloned.1.call-update) | async-done | bytes 8388624 | tf_op jit(solution)/shard_map/all_gather | solution.py:94
  381.5 7.7 %convolution_convert_fusion = bf16[512,256]{1,0:T(8,128)(2,1)} fusion(bf16[512,8192]{0,1:T(8,128)(2,1)} %all-gather.18.cloned.1.call-done, bf16[8192,256]{1,0:T(8,128)(2,1)} %all-gather.20.cloned.1.call-done), kind=kOutput, calls=%fused_computation.16 | convolution fusion | flops 2147614720 | bytes 12845056 | tf_op jit(solution)/shard_map/dot_general | solution.py:96
  (23 shorter events, 0.9 us)
Async XLA Ops:
  6.5 145.4 %copy-start.1 = (f32[8192]{0:T(1024)S(1)}, f32[8192]{0:T(1024)}, u32[]{:S(2)}) copy-start(f32[8192]{0:T(1024)} %param.7) | copy-start | bytes 98308
  6.5 109.7 %all-gather.8.cloned.1.call-start = ((), (), s32[]{:S(2)}) async-start(), calls=%async_computation | async-start | bytes 8650752 | tf_op jit(solution)/shard_map/all_gather | solution.py:36
  7.3 144.6 %all-gather.10.cloned.1.call-start = ((), (), s32[]{:S(2)}) async-start(), calls=%async_computation.1 | async-start | bytes 4718592 | tf_op jit(solution)/shard_map/all_gather | solution.py:55
  8.2 4.8 %collective-permute-start = (bf16[1024,2,32]{0,2,1:T(8,128)(2,1)S(1)}, bf16[1024,2,32]{0,2,1:T(8,128)(2,1)S(1)}, u32[]{:S(2)}, u32[]{:S(2)}) collective-permute-start(bf16[1024,2,32]{0,2,1:T(8,128)(2,1)S(1)} %pad_maximum_fusion.2), channel_id=1, source_target_pairs={{0,1},{1,0},{2,3},{3,2},{4,5},{5,4},{6,7},{7,6},{8,9},{9,8},{10,11... | collective-permute-start | bytes 393224 | tf_op jit(solution)/shard_map/ppermute | solution.py:10
  13.9 14.4 %collective-permute-start.1 = (bf16[1024,2,64]{0,2,1:T(8,128)(2,1)S(1)}, bf16[1024,2,64]{0,2,1:T(8,128)(2,1)S(1)}, u32[]{:S(2)}, u32[]{:S(2)}) collective-permute-start(bf16[1024,2,64]{0,2,1:T(8,128)(2,1)S(1)} %pad_maximum_fusion.1), channel_id=1, source_target_pairs={{0,2},{1,3},{2,0},{3,1},{4,6},{5,7},{6,4},{7,5},{8,10},{9,11},{10,... | collective-permute-start | bytes 786440 | tf_op jit(solution)/shard_map/ppermute | solution.py:10
  29.3 159.1 %all-gather.14.cloned.1.call-start = ((), (), s32[]{:S(2)}) async-start(), calls=%async_computation.3 | async-start | bytes 4718592 | tf_op jit(solution)/shard_map/all_gather | solution.py:50
  30.1 185.9 %all-gather.12.cloned.1.call-start = ((), (), s32[]{:S(2)}) async-start(), calls=%async_computation.2 | async-start | bytes 1179648 | tf_op jit(solution)/shard_map/all_gather | solution.py:68
  160.2 83.3 %all-gather.16.cloned.1.call-start = ((), (), s32[]{:S(2)}) async-start(), calls=%async_computation.4 | async-start | bytes 1179648 | tf_op jit(solution)/shard_map/all_gather | solution.py:69
  160.9 118.9 %all-gather.20.cloned.1.call-start = ((), (), s32[]{:S(2)}) async-start(), calls=%async_computation.6 | async-start | bytes 4718592 | tf_op jit(solution)/shard_map/all_gather | solution.py:97
  161.5 220.0 %all-gather.18.cloned.1.call-start = ((), (), s32[]{:S(2)}) async-start(), calls=%async_computation.5 | async-start | bytes 8650752 | tf_op jit(solution)/shard_map/all_gather | solution.py:94
  221.0 5.7 %copy-start = (f32[4096,512,2]{1,0,2:T(8,128)}, f32[4096,512,2]{1,0,2:T(8,128)S(1)}, u32[]{:S(2)}) copy-start(f32[4096,512,2]{1,0,2:T(8,128)S(1)} %get-tuple-element.18) | copy-start | bytes 50331652
Sparse Core Ops, SparseCore 0:
  9.8 106.3 all-gather.7
  118.1 33.7 all-gather.9
  153.8 34.6 all-gather.13
  190.1 25.7 all-gather.11
  217.6 25.7 all-gather.15
  245.2 34.6 all-gather.19
  282.5 98.9 all-gather.17
where the time goes:
time: 397 us; the launch traced here: 396 us
  waiting for transfers between devices  313 us (79%)
  matrix products  39 us (10%)
  other arithmetic  18.7 us (5%)
  between operations  13.6 us (3%)
  local copies, waits for them, and re-layouts  6.8 us (2%)
  starting transfers between devices  5.22 us (1%)
    all_gather x1, waiting for transfers between devices, per_device(): head_panel = lax.all_gather(heads, 'col', axis=1, tiled=True)  102 us
    all_gather x1, waiting for transfers between devices, per_device(): panel = lax.all_gather(hidden, 'col', axis=1, tiled=True)  86.1 us
    all_gather x1, waiting for transfers between devices, per_device(): lax.all_gather(stacked, 'row', axis=0, tiled=True)  30.5 us
    all_gather x1, waiting for transfers between devices, per_device(): lax.all_gather(wo, 'row', axis=0, tiled=True)  24.7 us
    all_gather x1, waiting for transfers between devices, per_device(): lax.all_gather(wq, 'row', axis=0, tiled=True)  23.2 us
    all_gather x1, waiting for transfers between devices, per_device(): key_piece = lax.all_gather(keys, 'row', axis=0, tiled=True)  17.6 us
    ppermute x2, waiting for transfers between devices, partner(): lax.ppermute(array, axis, [(i, i ^ 1 << distance) for i in range(lax.axis...  14.4 us
    all_gather x1, waiting for transfers between devices, per_device(): value_piece = lax.all_gather(values, 'row', axis=0, tiled=True)  12.6 us
  transfers between devices with their start and end apart: 9, of which 9 were waited for; matrix products, arithmetic and copies ran while one was open for 13% of the time, Pallas kernels for 0%

commit v1 on v0

v1 whole, which is shorter than its diff:
```python
import functools

import jax
import jax.numpy as jnp
from jax import lax
from jax.experimental import pallas as pl
from jax.experimental.pallas import tpu as pltpu
from jax.sharding import PartitionSpec as P

MESH = pl.DeviceIdType.MESH
BF = jnp.bfloat16
F32 = jnp.float32
HD = 128
TOK = 512
HALF = 256
COLS = 256
KROWS = 1024
NX, NY, NZ = 4, 4, 8
D = 8192
EXP2_SCALE = HD ** (-0.5) * 1.4426950408889634


def wait_bytes(ref, sem):
    pltpu.make_async_copy(ref, ref, sem).wait()


def kernel(
    hid, gain, wq, wkv, wo, ctab, stab, out,
    hbuf, wbuf, kvw, wob, acc, kvacc, ssacc, qs, qrx, kvs, kvrx, kvb, ssb, rcol, qb, hb, osb, orx,
    t_s, t_r, z_s, z_r, g_s, g_r, y_s, y_r, yk_s, yk_r, yo_s, yo_r,
    c_s, c_r, loc, q_s, q_r, ss_s, ss_r, k_s, k_r, b_s, b_r, p_s, p_r, o_s, o_r,
):
    row = lax.axis_index("row")
    col = lax.axis_index("col")
    x, core = row // 2, row % 2
    y, z = col // NZ, col % NZ
    g, zq = z // 4, z % 4
    d = 2 * y + core
    prow = row + 1 - 2 * core

    def remote(src, dst, ss, rs, r, c):
        return pltpu.make_async_remote_copy(
            src_ref=src, dst_ref=dst, send_sem=ss, recv_sem=rs, device_id=(r, c), device_id_type=MESH
        )

    zr, zl = 8 * y + (z + 1) % NZ, 8 * y + (z + NZ - 1) % NZ
    yr, yl = 8 * ((y + 1) % NY) + z, 8 * ((y + NY - 1) % NY) + z
    low = row < 4
    t_y = jnp.where(low, row, 7 - row)

    barrier = pltpu.get_barrier_semaphore()

    def greet(r, c):
        pl.semaphore_signal(barrier, inc=1, device_id=(r, c), device_id_type=MESH)

    def greet_maybe_self(r, c):
        me = jnp.logical_and(r == row, c == col)

        @pl.when(jnp.logical_not(me))
        def _():
            greet(r, c)

        return jnp.where(me, 0, 1)

    count = 0
    for c in (zr, zl, yr, yl):
        greet(row, c)
        count += 1
    greet(prow, col)
    count += 1
    count += greet_maybe_self(y, 8 * x + z)
    count += greet_maybe_self(7 - y, 8 * x + z)
    for dx in range(4):
        for dj in range(4):
            if dx or dj:
                greet(2 * ((x + dx) % NX) + core, 8 * y + 4 * g + (zq + dj) % 4)
                count += 1
    for dy in range(1, 4):
        for dj in range(4):
            greet(row, 8 * ((y + dy) % NY) + 4 * g + (zq + dj) % 4)
            count += 1
    for xs in range(4):
        for cs in range(2):
            count += greet_maybe_self(2 * xs + cs, 8 * t_y + z)

    own = [
        pltpu.make_async_copy(wq, wbuf.at[core, y], loc.at[0]),
        pltpu.make_async_copy(wkv, kvw.at[core, :, pl.ds(pl.multiple_of(128 * y, 128), 128)], loc.at[1]),
        pltpu.make_async_copy(wo, wob.at[core, y], loc.at[2]),
    ]
    for c in own:
        c.start()
    acc[...] = jnp.zeros_like(acc)
    kvacc[...] = jnp.zeros_like(kvacc)
    ssacc[...] = jnp.zeros_like(ssacc)
    pl.semaphore_wait(barrier, count)

    t_copies = []
    for h in range(2):
        tcore = jnp.where(low, h, 1 - h)
        slot = jnp.where(low, 0, 1)
        tr, tc = 2 * y + tcore, 8 * t_y + z
        me = jnp.logical_and(tr == row, tc == col)
        src = hid.at[pl.ds(HALF * h, HALF)]
        dst = hbuf.at[z, pl.ds(pl.multiple_of(HALF * slot, HALF), HALF)]
        cp = remote(src, dst, t_s.at[h], t_r.at[slot], tr, tc)
        t_copies.append((cp, me))

        @pl.when(me)
        def _():
            pltpu.make_async_copy(src, dst, t_r.at[slot]).start()

        @pl.when(jnp.logical_not(me))
        def _():
            cp.start()

    sends = []

    def go(cp):
        cp.start()
        sends.append(cp)

    kl = pl.ds(pl.multiple_of(128 * y, 128), 128)
    go(remote(wq, wbuf.at[core, y], y_s.at[0, 0], y_r.at[0, 0], row, yr))
    go(remote(wq, wbuf.at[core, y], y_s.at[1, 0], y_r.at[1, 0], row, yl))
    go(remote(wkv, kvw.at[core, :, kl], yk_s.at[0, 0], yk_r.at[0, 0], row, yr))
    go(remote(wkv, kvw.at[core, :, kl], yk_s.at[1, 0], yk_r.at[1, 0], row, yl))
    go(remote(wq, wbuf.at[core, y], c_s.at[0], c_r.at[0], prow, col))
    go(remote(wkv, kvw.at[core, :, kl], c_s.at[0], c_r.at[1], prow, col))

    def ring_send(buf, ss, rs, s, h):
        hs = pl.ds(HALF * h, HALF)
        a = (z + NZ - s) % NZ
        b = (z + s) % NZ
        if s < 3 or h == 0:
            go(remote(buf.at[a, hs], buf.at[a, hs], ss.at[0, s, h], rs.at[0, s, h], row, zr))
        if s < 3 or h == 1:
            go(remote(buf.at[b, hs], buf.at[b, hs], ss.at[1, s, h], rs.at[1, s, h], row, zl))

    def ring_wait(buf, rs, s, h):
        hs = pl.ds(HALF * h, HALF)
        if s < 3 or h == 0:
            wait_bytes(buf.at[(z + NZ - s - 1) % NZ, hs], rs.at[0, s, h])
        if s < 3 or h == 1:
            wait_bytes(buf.at[(z + s + 1) % NZ, hs], rs.at[1, s, h])

    def ring_step(buf, ss, rs, s):
        for h in range(2):
            ring_wait(buf, rs, s, h)
            if s < 3:
                ring_send(buf, ss, rs, s + 1, h)

    for h in range(2):
        wait_bytes(hbuf.at[z, pl.ds(HALF * h, HALF)], t_r.at[h])
        ring_send(hbuf, z_s, z_r, 0, h)

    ring_step(hbuf, z_s, z_r, 0)

    y1, y3, y2 = (y + 1) % NY, (y + 3) % NY, (y + 2) % NY

    def weight_hop(buf, sems, rsems, c_sem, half_rows):
        wait_bytes(buf.at[core, y3], rsems.at[0, 0])
        go(remote(buf.at[core, y3, pl.ds(0, half_rows)], buf.at[core, y3, pl.ds(0, half_rows)],
                  sems.at[0, 1], rsems.at[0, 1], row, yr))
        wait_bytes(buf.at[core, y1], rsems.at[1, 0])
        go(remote(buf.at[core, y1, pl.ds(half_rows, half_rows)], buf.at[core, y1, pl.ds(half_rows, half_rows)],
                  sems.at[1, 1], rsems.at[1, 1], row, yl))
        for b in (y3, y1):
            go(remote(buf.at[core, b], buf.at[core, b], c_s.at[0], c_sem, prow, col))

    def weight_last(buf, rsems, c_sem, half_rows):
        wait_bytes(buf.at[core, y2, pl.ds(0, half_rows)], rsems.at[0, 1])
        wait_bytes(buf.at[core, y2, pl.ds(half_rows, half_rows)], rsems.at[1, 1])
        go(remote(buf.at[core, y2], buf.at[core, y2], c_s.at[0], c_sem, prow, col))

    def lanes(b):
        return pl.ds(pl.multiple_of(128 * b, 128), 128)

    weight_hop(wbuf, y_s, y_r, c_r.at[0], KROWS // 2)
    l3, l1, l2 = lanes(y3), lanes(y1), lanes(y2)
    top, bot = pl.ds(0, 256), pl.ds(256, 256)
    wait_bytes(kvw.at[core, :, l3], yk_r.at[0, 0])
    go(remote(kvw.at[core, top, l3], kvw.at[core, top, l3], yk_s.at[0, 1], yk_r.at[0, 1], row, yr))
    wait_bytes(kvw.at[core, :, l1], yk_r.at[1, 0])
    go(remote(kvw.at[core, bot, l1], kvw.at[core, bot, l1], yk_s.at[1, 1], yk_r.at[1, 1], row, yl))
    for b in (l3, l1):
        go(remote(kvw.at[core, :, b], kvw.at[core, :, b], c_s.at[0], c_r.at[1], prow, col))

    ring_step(hbuf, z_s, z_r, 1)

    weight_last(wbuf, y_r, c_r.at[0], KROWS // 2)
    wait_bytes(kvw.at[core, top, l2], yk_r.at[0, 1])
    wait_bytes(kvw.at[core, bot, l2], yk_r.at[1, 1])
    go(remote(kvw.at[core, :, l2], kvw.at[core, :, l2], c_s.at[0], c_r.at[1], prow, col))

    go(remote(wo, wob.at[core, y], yo_s.at[0, 0], yo_r.at[0, 0], row, yr))
    go(remote(wo, wob.at[core, y], yo_s.at[1, 0], yo_r.at[1, 0], row, yl))
    go(remote(wo, wob.at[core, y], c_s.at[0], c_r.at[2], prow, col))

    other = 1 - core
    wait_bytes(wbuf.at[other], c_r.at[0])
    wait_bytes(kvw.at[other], c_r.at[1])
    for c in own:
        c.wait()

    lane512 = lax.broadcasted_iota(jnp.int32, (TOK, 512), 1) % 128 // 64

    def project(zi):
        at = pl.multiple_of(2048 * x + COLS * zi, COLS)
        hv = hbuf[zi].astype(F32)
        sq = hv * hv
        ssacc[...] += sq[:, :128] + sq[:, 128:]
        hg = (hv * gain[:, pl.ds(at, COLS)]).astype(BF)
        kr = pl.ds(pl.multiple_of(zi % 4 * 256, 256), 256)
        for b in range(4):
            acc[b] += jnp.dot(hg, wbuf[zi // 4, b, kr, :], preferred_element_type=F32)
        kk = pl.ds(pl.multiple_of(zi % 2 * 256, 256), 256)
        part = jnp.dot(hg, kvw[zi // 4, kk, :], preferred_element_type=F32)
        kvacc[...] += jnp.where(lane512 == zi % 4 // 2, part, 0.0)

    def near(i, _):
        project((z + NZ - 2 + i) % NZ)
        return 0

    lax.fori_loop(0, 5, near, 0)
    ring_step(hbuf, z_s, z_r, 2)

    def far(i, _):
        project((z + 3 + 2 * i) % NZ)
        return 0

    lax.fori_loop(0, 2, far, 0)
    ring_step(hbuf, z_s, z_r, 3)
    project((z + 4) % NZ)

    for dx in range(4):
        xt = (x + dx) % NX
        kvs[dx] = kvacc[:, lanes(xt)].astype(BF)
        for dj in range(4):
            jq = (zq + dj) % 4
            piece = kvs.at[dx, pl.ds(pl.multiple_of(128 * jq, 128), 128)]
            slot = (4 - dx) % 4 * 4 + (4 - dj) % 4
            if slot == 0:
                kvrx[0] = kvs[dx, pl.ds(pl.multiple_of(128 * jq, 128), 128), :]
            else:
                go(remote(piece, kvrx.at[slot], k_s.at[0], k_r.at[0], 2 * xt + core, 8 * y + 4 * g + jq))
    ssb[0] = lax.dot_general(
        jnp.ones((8, 128), F32), ssacc[...], (((1,), (1,)), ((), ())),
        precision=lax.Precision.HIGHEST, preferred_element_type=F32,
    )
    for dx in range(1, 4):
        go(remote(ssb.at[0], ssb.at[dx], ss_s.at[0], ss_r.at[0], 2 * ((x + dx) % NX) + core, col))
    for dx in range(1, 4):
        xt = (x + dx) % NX
        qs[dx - 1] = acc[xt].astype(BF)
        go(remote(qs.at[dx - 1], qrx.at[dx - 1], q_s.at[0], q_r.at[0], 2 * xt + core, col))

    wait_bytes(ssb.at[pl.ds(1, 3)], ss_r.at[0])
    total = ssb[0] + ssb[1] + ssb[2] + ssb[3]
    r8 = lax.rsqrt(total / D + 1e-05)
    rcol[...] = lax.dot_general(
        r8, jnp.full((8, 128), 0.125, F32), (((0,), (0,)), ((), ())),
        precision=lax.Precision.HIGHEST, preferred_element_type=F32,
    )

    wait_bytes(kvrx.at[pl.ds(1, 15)], k_r.at[0])
    mine = pl.ds(pl.multiple_of(128 * zq, 128), 128)
    lane = lax.broadcasted_iota(jnp.int32, (128, 128), 1) // 32
    keys = jnp.zeros((128, 128), F32)
    vals = jnp.zeros((128, 128), F32)
    for j in range(4):
        dj = (j + 4 - zq) % 4
        part = kvrx[dj].astype(F32)
        for dx in range(1, 4):
            part += kvrx[4 * dx + dj].astype(F32)
        part = part + pltpu.roll(part, 64, 1)
        keys = jnp.where(lane == j, part if j % 2 == 0 else pltpu.roll(part, 32, 1), keys)
        vals = jnp.where(lane == j, part if j % 2 == 1 else pltpu.roll(part, 96, 1), vals)
    keys = keys * rcol[mine, :]
    vals = vals * rcol[mine, :]
    keys = keys * ctab[mine, :] + pltpu.roll(keys, 64, 1) * stab[mine, :]

    def block_at(yy, jj):
        dd = 2 * yy + core
        return jnp.where(jj < 2, 2 * dd, 2 * (15 - dd)) + jj % 2

    here = block_at(y, zq)
    kvb[here, :, 0:128] = keys.astype(BF)
    kvb[here, :, 128:256] = vals.astype(BF)
    peers = []
    for dy in range(4):
        for dj in range(4):
            if dy or dj:
                yy, jj = (y + dy) % NY, (zq + dj) % 4
                peers.append((yy, jj))
                go(remote(kvb.at[here], kvb.at[here], b_s.at[0], b_r.at[0], row, 8 * yy + 4 * g + jj))
    go(remote(kvb.at[here], kvb.at[here], p_s.at[0], p_r.at[0], prow, col))

    wait_bytes(qrx, q_r.at[0])
    for h in range(2):
        hl = slice(128 * h, 128 * h + 128)
        q = acc[x, :, hl]
        for i in range(3):
            q += qrx[i, :, hl].astype(F32)
        q = q * rcol[...]
        q = (q * ctab[...] + pltpu.roll(q, 64, 1) * stab[...]).astype(BF)
        for k in range(2):
            qb[k, HALF * h : HALF * (h + 1), :] = q[HALF * k : HALF * (k + 1), :]

    weight_hop(wob, yo_s, yo_r, c_r.at[2], KROWS // 2)

    wait_bytes(kvb.at[pl.ds(0, 15)], b_r.at[0])
    for yy, jj in peers:
        b = block_at(yy, jj)
        go(remote(kvb.at[b], kvb.at[b], p_s.at[0], p_r.at[0], prow, col))
    wait_bytes(kvb.at[pl.ds(0, 16)], p_r.at[0])

    rows = 2 * HALF
    tri = (
        lax.broadcasted_iota(jnp.int32, (rows, HALF), 0) % HALF
        >= lax.broadcasted_iota(jnp.int32, (rows, HALF), 1)
    )

    for k in range(2):
        qk = qb[k]

        def scores(t):
            key = kvb[pl.ds(2 * t, 2), :, 0:128].reshape(HALF, 128)
            val = kvb[pl.ds(2 * t, 2), :, 128:256].reshape(HALF, 128)
            s = lax.dot_general(qk, key, (((1,), (1,)), ((), ())), preferred_element_type=F32)
            return s * EXP2_SCALE, val

        last = d if k == 0 else 15 - d
        s, val = scores(last)
        s = jnp.where(tri, s, -jnp.inf)
        top_ = jnp.max(s, axis=1, keepdims=True)
        p = jnp.exp2(s - top_)
        den = jnp.sum(p, axis=1, keepdims=True)
        num = jnp.dot(p.astype(BF), val, preferred_element_type=F32)

        def step(t, carry):
            top_, den, num = carry
            s, val = scores(t)
            new = jnp.maximum(top_, jnp.max(s, axis=1, keepdims=True))
            fix = jnp.exp2(top_ - new)
            p = jnp.exp2(s - new)
            den = den * fix + jnp.sum(p, axis=1, keepdims=True)
            num = num * fix + jnp.dot(p.astype(BF), val, preferred_element_type=F32)
            return new, den, num

        top_, den, num = lax.fori_loop(0, last, step, (top_, den, num))
        res = (num / den).astype(BF)
        for h in range(2):
            hb[z, HALF * k : HALF * (k + 1), 128 * h : 128 * (h + 1)] = res[HALF * h : HALF * (h + 1), :]
        ring_send(hb, g_s, g_r, 0, k)

    ring_step(hb, g_s, g_r, 0)
    weight_last(wob, yo_r, c_r.at[2], KROWS // 2)
    ring_step(hb, g_s, g_r, 1)
    wait_bytes(wob.at[other], c_r.at[2])
    acc[...] = jnp.zeros_like(acc)

    def finish(zi):
        hg = hb[zi]
        kr = pl.ds(pl.multiple_of(zi % 4 * 256, 256), 256)
        for b in range(4):
            acc[b] += jnp.dot(hg, wob[zi // 4, b, kr, :], preferred_element_type=F32)

    def near_out(i, _):
        finish((z + NZ - 2 + i) % NZ)
        return 0

    lax.fori_loop(0, 5, near_out, 0)
    ring_step(hb, g_s, g_r, 2)

    def far_out(i, _):
        finish((z + 3 + 2 * i) % NZ)
        return 0

    lax.fori_loop(0, 2, far_out, 0)
    ring_step(hb, g_s, g_r, 3)
    finish((z + 4) % NZ)

    o_copies = []
    for b in range(4):
        osb[b] = acc[b].astype(BF)
        for k in range(2):
            tr = y if k == 0 else 7 - y
            ha = core if k == 0 else 1 - core
            me = jnp.logical_and(tr == row, b == y)
            src = osb.at[b, pl.ds(HALF * k, HALF)]
            dst = orx.at[x, ha]
            rs = o_r.at[2 * x + ha]
            cp = remote(src, dst, o_s.at[2 * b + k], rs, tr, 8 * b + z)
            o_copies.append((cp, me))

            @pl.when(me)
            def _():
                pltpu.make_async_copy(src, dst, rs).start()

            @pl.when(jnp.logical_not(me))
            def _():
                cp.start()

    for ha in range(2):
        for xs in range(4):
            wait_bytes(orx.at[xs, ha], o_r.at[2 * xs + ha])
        v = orx[0, ha].astype(F32)
        for xs in range(1, 4):
            v += orx[xs, ha].astype(F32)
        out[HALF * ha : HALF * (ha + 1), :] = v.astype(BF)

    for cp in sends:
        cp.wait_send()
    for cp, me in t_copies + o_copies:

        @pl.when(jnp.logical_not(me))
        def _():
            cp.wait_send()


def per_device(hidden, norm_gain, wq, wk, wv, wo):
    row, col = lax.axis_index("row"), lax.axis_index("col")
    d = 2 * (col // NZ) + row % 2
    i = jnp.arange(TOK)
    positions = jnp.where(i < HALF, HALF * d + i, HALF * (15 - d) + i - HALF)
    steps = jnp.arange(HD // 2).astype(F32)
    freqs = 10000.0 ** (-steps / (HD // 2))
    angles = positions.astype(F32)[:, None] * freqs[None, :]
    cosine, sine = jnp.cos(angles), jnp.sin(angles)
    ctab = jnp.concatenate([cosine, cosine], axis=1)
    stab = jnp.concatenate([-sine, sine], axis=1)
    both = jnp.concatenate([wk, wv], axis=1)
    wkv = jnp.concatenate([both[:512], both[512:]], axis=1)
    dma = pltpu.SemaphoreType.DMA
    vmem = pl.BlockSpec(memory_space=pltpu.VMEM)
    anyw = pl.BlockSpec(memory_space=pl.ANY)
    scratch = [
        pltpu.VMEM((NZ, TOK, COLS), BF),
        pltpu.VMEM((2, NY, KROWS, COLS), BF),
        pltpu.VMEM((2, 512, 512), BF),
        pltpu.VMEM((2, NY, KROWS, COLS), BF),
        pltpu.VMEM((NY, TOK, COLS), F32),
        pltpu.VMEM((TOK, 512), F32),
        pltpu.VMEM((TOK, 128), F32),
        pltpu.VMEM((3, TOK, COLS), BF),
        pltpu.VMEM((3, TOK, COLS), BF),
        pltpu.VMEM((4, TOK, 128), BF),
        pltpu.VMEM((16, 128, 128), BF),
        pltpu.VMEM((32, 128, 256), BF),
        pltpu.VMEM((4, 8, TOK), F32),
        pltpu.VMEM((TOK, 128), F32),
        pltpu.VMEM((2, TOK, 128), BF),
        pltpu.VMEM((NZ, TOK, COLS), BF),
        pltpu.VMEM((NY, TOK, COLS), BF),
        pltpu.VMEM((4, 2, HALF, COLS), BF),
        dma((2,)), dma((2,)),
        dma((2, 4, 2)), dma((2, 4, 2)),
        dma((2, 4, 2)), dma((2, 4, 2)),
        dma((2, 2)), dma((2, 2)),
        dma((2, 2)), dma((2, 2)),
        dma((2, 2)), dma((2, 2)),
        dma((1,)), dma((3,)),
        dma((3,)),
        dma((1,)), dma((1,)),
        dma((1,)), dma((1,)),
        dma((1,)), dma((1,)),
        dma((1,)), dma((1,)),
        dma((1,)), dma((1,)),
        dma((8,)), dma((8,)),
    ]
    return pl.pallas_call(
        kernel,
        out_shape=jax.ShapeDtypeStruct((TOK, COLS), BF),
        in_specs=[anyw, vmem, anyw, anyw, anyw, vmem, vmem],
        out_specs=vmem,
        scratch_shapes=scratch,
        compiler_params=pltpu.CompilerParams(
            collective_id=0, has_side_effects=True, vmem_limit_bytes=56 * 1024 * 1024
        ),
    )(hidden, norm_gain.reshape(1, D), wq, wkv, wo, ctab, stab)


def solution(mesh):
    spec = P("row", "col")
    return jax.shard_map(
        per_device, mesh=mesh, in_specs=(spec, P(), spec, spec, spec, spec), out_specs=spec, check_vma=False
    )
```

time: 397 us -> 169 us (0.43)
  the two profiles are of different devices: /device:TPU:5 before, /device:TPU:30 now
where the time goes in v1:
time: 169 us; the launch traced here: 168 us
  Pallas kernels  163 us (96%)
  other arithmetic  2.89 us (2%)
  local copies, waits for them, and re-layouts  2.68 us (2%)
    pallas_call x1, Pallas kernels, per_device(): pl.pallas_call(kernel, out_shape=jax.ShapeDtypeStruct((TOK, COLS), BF), i...  163 us

profile of v1, /device:TPU:30, one launch (start us, length us, event | category | flops | bytes accessed | tf_op | source)
XLA Modules:
  0.0 168.5 jit_solution(3387832470762033945)
XLA Ops:
  0.0 1.0 fusion.2
  1.0 0.0 copy-start
  1.0 1.0 pad_maximum_fusion
  2.0 0.0 copy-done
  2.0 0.0 copy-start.1
  2.0 0.2 copy.7
  2.2 0.7 copy-done.1
  2.9 0.2 copy.8
  3.0 0.1 fusion
  3.1 0.8 fusion.1.wkv
  3.9 162.9 %shard_map.64 = bf16[512,256]{1,0:T(8,128)(2,1)} custom-call(bf16[512,256]{1,0:T(8,128)(2,1)} %hid.1, f32[1,8192]{1,0:T(1,128)} %bitcast.1, bf16[1024,256]{1,0:T(8,128)(2,1)} %wq.1, bf16[512,128]{1,0:T(8,128)(2,1)} %fusion.1.wkv, bf16[1024,256]{1,0:T(8,128)(2,1)} %wo.1, f32[512,128]{1,0:T(8,128)} %get-tuple-element.8.ctab, f32[512,128]{1,0:T(8,128)} %get-tuple-element.9.stab), custom_call_target="tpu_custom_call" | custom-call | tf_op jit(solution)/shard_map/pallas_call | solution.py:472
  166.8 1.7 copy.10
  (2 shorter events, 0.0 us)
Async XLA Ops:
  1.0 1.0 copy-start
  2.0 0.8 copy-start.1

commit v2 on v1

--- a/solution.py
+++ b/solution.py
@@ -26,9 +26,9 @@
 
 def kernel(
     hid, gain, wq, wkv, wo, ctab, stab, out,
-    hbuf, wbuf, kvw, wob, acc, kvacc, ssacc, qs, qrx, kvs, kvrx, kvb, ssb, rcol, qb, hb, osb, orx,
+    hbuf, wbuf, kvw, wob, acc, kvacc, ssacc, qs, qrx, kvs, kvrx, kvb, ssb, rcol, qb, hb, osb, orx, fin, frx,
     t_s, t_r, z_s, z_r, g_s, g_r, y_s, y_r, yk_s, yk_r, yo_s, yo_r,
-    c_s, c_r, loc, q_s, q_r, ss_s, ss_r, k_s, k_r, b_s, b_r, p_s, p_r, o_s, o_r,
+    c_s, c_r, loc, q_s, q_r, ss_s, ss_r, k_s, k_r, b_s, b_r, bl_r, br_r, bf_r, p_s, p_r, o_s, o_r, f_s, f_r,
 ):
     row = lax.axis_index("row")
     col = lax.axis_index("col")
@@ -75,13 +75,8 @@
             if dx or dj:
                 greet(2 * ((x + dx) % NX) + core, 8 * y + 4 * g + (zq + dj) % 4)
                 count += 1
-    for dy in range(1, 4):
-        for dj in range(4):
-            greet(row, 8 * ((y + dy) % NY) + 4 * g + (zq + dj) % 4)
-            count += 1
-    for xs in range(4):
-        for cs in range(2):
-            count += greet_maybe_self(2 * xs + cs, 8 * t_y + z)
+    for cs in range(2):
+        count += greet_maybe_self(2 * y + cs, 8 * t_y + z)
 
     own = [
         pltpu.make_async_copy(wq, wbuf.at[core, y], loc.at[0]),
@@ -144,17 +139,16 @@
         if s < 3 or h == 1:
             wait_bytes(buf.at[(z + s + 1) % NZ, hs], rs.at[1, s, h])
 
-    def ring_step(buf, ss, rs, s):
-        for h in range(2):
-            ring_wait(buf, rs, s, h)
-            if s < 3:
-                ring_send(buf, ss, rs, s + 1, h)
+    def ring_step(buf, ss, rs, s, h):
+        ring_wait(buf, rs, s, h)
+        if s < 3:
+            ring_send(buf, ss, rs, s + 1, h)
 
     for h in range(2):
         wait_bytes(hbuf.at[z, pl.ds(HALF * h, HALF)], t_r.at[h])
         ring_send(hbuf, z_s, z_r, 0, h)
 
-    ring_step(hbuf, z_s, z_r, 0)
+    ring_step(hbuf, z_s, z_r, 0, 0)
 
     y1, y3, y2 = (y + 1) % NY, (y + 3) % NY, (y + 2) % NY
 
@@ -177,6 +171,8 @@
         return pl.ds(pl.multiple_of(128 * b, 128), 128)
 
     weight_hop(wbuf, y_s, y_r, c_r.at[0], KROWS // 2)
+    ring_step(hbuf, z_s, z_r, 1, 0)
+    ring_step(hbuf, z_s, z_r, 0, 1)
     l3, l1, l2 = lanes(y3), lanes(y1), lanes(y2)
     top, bot = pl.ds(0, 256), pl.ds(256, 256)
     wait_bytes(kvw.at[core, :, l3], yk_r.at[0, 0])
@@ -186,7 +182,8 @@
     for b in (l3, l1):
         go(remote(kvw.at[core, :, b], kvw.at[core, :, b], c_s.at[0], c_r.at[1], prow, col))
 
-    ring_step(hbuf, z_s, z_r, 1)
+    ring_step(hbuf, z_s, z_r, 2, 0)
+    ring_step(hbuf, z_s, z_r, 1, 1)
 
     weight_last(wbuf, y_r, c_r.at[0], KROWS // 2)
     wait_bytes(kvw.at[core, top, l2], yk_r.at[0, 1])
@@ -198,62 +195,84 @@
     go(remote(wo, wob.at[core, y], c_s.at[0], c_r.at[2], prow, col))
 
     other = 1 - core
+    ring_step(hbuf, z_s, z_r, 3, 0)
+    ring_step(hbuf, z_s, z_r, 2, 1)
     wait_bytes(wbuf.at[other], c_r.at[0])
     wait_bytes(kvw.at[other], c_r.at[1])
     for c in own:
         c.wait()
 
-    lane512 = lax.broadcasted_iota(jnp.int32, (TOK, 512), 1) % 128 // 64
-
-    def project(zi):
+    lane512 = lax.broadcasted_iota(jnp.int32, (HALF, 512), 1) % 128 // 64
+
+    def project(zi, h):
+        hs = pl.ds(HALF * h, HALF)
         at = pl.multiple_of(2048 * x + COLS * zi, COLS)
-        hv = hbuf[zi].astype(F32)
+        hv = hbuf[zi, hs].astype(F32)
         sq = hv * hv
-        ssacc[...] += sq[:, :128] + sq[:, 128:]
+        ssacc[hs] += sq[:, :128] + sq[:, 128:]
         hg = (hv * gain[:, pl.ds(at, COLS)]).astype(BF)
         kr = pl.ds(pl.multiple_of(zi % 4 * 256, 256), 256)
         for b in range(4):
-            acc[b] += jnp.dot(hg, wbuf[zi // 4, b, kr, :], preferred_element_type=F32)
+            acc[b, hs] += jnp.dot(hg, wbuf[zi // 4, b, kr, :], preferred_element_type=F32)
         kk = pl.ds(pl.multiple_of(zi % 2 * 256, 256), 256)
         part = jnp.dot(hg, kvw[zi // 4, kk, :], preferred_element_type=F32)
-        kvacc[...] += jnp.where(lane512 == zi % 4 // 2, part, 0.0)
-
-    def near(i, _):
-        project((z + NZ - 2 + i) % NZ)
+        kvacc[hs] += jnp.where(lane512 == zi % 4 // 2, part, 0.0)
+
+    k_copies = []
+
+    def reduce_kv(h):
+        hs = pl.ds(HALF * h, HALF)
+        for dx in range(4):
+            xt = (x + dx) % NX
+            kvs[dx, hs] = kvacc[hs, lanes(xt)].astype(BF)
+            for jq in (2 * h, 2 * h + 1):
+                piece = kvs.at[dx, pl.ds(128 * jq, 128)]
+                dst = kvrx.at[(4 - dx) % 4 * 4 + (zq + 4 - jq) % 4]
+                cp = remote(piece, dst, k_s.at[0], k_r.at[0], 2 * xt + core, 8 * y + 4 * g + jq)
+                if dx:
+                    go(cp)
+                else:
+                    me = zq == jq
+                    k_copies.append((cp, me))
+
+                    @pl.when(me)
+                    def _():
+                        pltpu.make_async_copy(piece, dst, k_r.at[0]).start()
+
+                    @pl.when(jnp.logical_not(me))
+                    def _():
+                        cp.start()
+
+    def reduce_q(h):
+        hs = pl.ds(HALF * h, HALF)
+        for dx in range(1, 4):
+            xt = (x + dx) % NX
+            qs[dx - 1, hs] = acc[xt, hs].astype(BF)
+            go(remote(qs.at[dx - 1, hs], qrx.at[dx - 1, hs], q_s.at[0], q_r.at[0], 2 * xt + core, col))
+
+    def first_half(i, _):
+        project(i, 0)
         return 0
 
-    lax.fori_loop(0, 5, near, 0)
-    ring_step(hbuf, z_s, z_r, 2)
-
-    def far(i, _):
-        project((z + 3 + 2 * i) % NZ)
+    def second_half(i, _):
+        project((z + NZ - 3 + i) % NZ, 1)
         return 0
 
-    lax.fori_loop(0, 2, far, 0)
-    ring_step(hbuf, z_s, z_r, 3)
-    project((z + 4) % NZ)
-
-    for dx in range(4):
-        xt = (x + dx) % NX
-        kvs[dx] = kvacc[:, lanes(xt)].astype(BF)
-        for dj in range(4):
-            jq = (zq + dj) % 4
-            piece = kvs.at[dx, pl.ds(pl.multiple_of(128 * jq, 128), 128)]
-            slot = (4 - dx) % 4 * 4 + (4 - dj) % 4
-            if slot == 0:
-                kvrx[0] = kvs[dx, pl.ds(pl.multiple_of(128 * jq, 128), 128), :]
-            else:
-                go(remote(piece, kvrx.at[slot], k_s.at[0], k_r.at[0], 2 * xt + core, 8 * y + 4 * g + jq))
+    lax.fori_loop(0, NZ, first_half, 0)
+    reduce_kv(0)
+    reduce_q(0)
+    weight_hop(wob, yo_s, yo_r, c_r.at[2], KROWS // 2)
+    lax.fori_loop(0, 7, second_half, 0)
+    ring_step(hbuf, z_s, z_r, 3, 1)
+    project((z + 4) % NZ, 1)
+    reduce_kv(1)
     ssb[0] = lax.dot_general(
         jnp.ones((8, 128), F32), ssacc[...], (((1,), (1,)), ((), ())),
         precision=lax.Precision.HIGHEST, preferred_element_type=F32,
     )
     for dx in range(1, 4):
         go(remote(ssb.at[0], ssb.at[dx], ss_s.at[0], ss_r.at[0], 2 * ((x + dx) % NX) + core, col))
-    for dx in range(1, 4):
-        xt = (x + dx) % NX
-        qs[dx - 1] = acc[xt].astype(BF)
-        go(remote(qs.at[dx - 1], qrx.at[dx - 1], q_s.at[0], q_r.at[0], 2 * xt + core, col))
+    reduce_q(1)
 
     wait_bytes(ssb.at[pl.ds(1, 3)], ss_r.at[0])
     total = ssb[0] + ssb[1] + ssb[2] + ssb[3]
@@ -263,7 +282,7 @@
         precision=lax.Precision.HIGHEST, preferred_element_type=F32,
     )
 
-    wait_bytes(kvrx.at[pl.ds(1, 15)], k_r.at[0])
+    wait_bytes(kvrx, k_r.at[0])
     mine = pl.ds(pl.multiple_of(128 * zq, 128), 128)
     lane = lax.broadcasted_iota(jnp.int32, (128, 128), 1) // 32
     keys = jnp.zeros((128, 128), F32)
@@ -287,14 +306,35 @@
     here = block_at(y, zq)
     kvb[here, :, 0:128] = keys.astype(BF)
     kvb[here, :, 128:256] = vals.astype(BF)
-    peers = []
-    for dy in range(4):
-        for dj in range(4):
-            if dy or dj:
-                yy, jj = (y + dy) % NY, (zq + dj) % 4
-                peers.append((yy, jj))
-                go(remote(kvb.at[here], kvb.at[here], b_s.at[0], b_r.at[0], row, 8 * yy + 4 * g + jj))
-    go(remote(kvb.at[here], kvb.at[here], p_s.at[0], p_r.at[0], prow, col))
+    kv_here = [block_at(y, (zq + dj) % 4) for dj in range(4)]
+    kv_left = [block_at(y3, (zq + dj) % 4) for dj in range(4)]
+    kv_right = [block_at(y1, (zq + dj) % 4) for dj in range(4)]
+    kv_far = [block_at(y2, (zq + dj) % 4) for dj in range(4)]
+    half0, half1 = pl.ds(0, 64), pl.ds(64, 64)
+
+    def to_partner(b):
+        go(remote(kvb.at[b], kvb.at[b], p_s.at[0], p_r.at[0], prow, col))
+
+    def kv_hop(dj):
+        b = kv_here[dj]
+        go(remote(kvb.at[b], kvb.at[b], b_s.at[0], bl_r.at[dj], row, yr))
+        go(remote(kvb.at[b], kvb.at[b], b_s.at[0], br_r.at[dj], row, yl))
+        to_partner(b)
+
+    for dj in (1, 3, 2):
+        go(remote(kvb.at[here], kvb.at[here], b_s.at[0], b_r.at[4 - dj], row, 8 * y + 4 * g + (zq + dj) % 4))
+    kv_hop(0)
+    for dj in (1, 3, 2):
+        wait_bytes(kvb.at[kv_here[dj]], b_r.at[dj])
+        kv_hop(dj)
+    for dj in (0, 1, 3, 2):
+        left, right = kv_left[dj], kv_right[dj]
+        wait_bytes(kvb.at[left], bl_r.at[dj])
+        go(remote(kvb.at[left, half0], kvb.at[left, half0], b_s.at[0], bf_r.at[0, dj], row, yr))
+        wait_bytes(kvb.at[right], br_r.at[dj])
+        go(remote(kvb.at[right, half1], kvb.at[right, half1], b_s.at[0], bf_r.at[1, dj], row, yl))
+        to_partner(left)
+        to_partner(right)
 
     wait_bytes(qrx, q_r.at[0])
     for h in range(2):
@@ -307,12 +347,12 @@
         for k in range(2):
             qb[k, HALF * h : HALF * (h + 1), :] = q[HALF * k : HALF * (k + 1), :]
 
-    weight_hop(wob, yo_s, yo_r, c_r.at[2], KROWS // 2)
-
-    wait_bytes(kvb.at[pl.ds(0, 15)], b_r.at[0])
-    for yy, jj in peers:
-        b = block_at(yy, jj)
-        go(remote(kvb.at[b], kvb.at[b], p_s.at[0], p_r.at[0], prow, col))
+
+    for dj in (0, 1, 3, 2):
+        far = kv_far[dj]
+        wait_bytes(kvb.at[far, half0], bf_r.at[0, dj])
+        wait_bytes(kvb.at[far, half1], bf_r.at[1, dj])
+        to_partner(far)
     wait_bytes(kvb.at[pl.ds(0, 16)], p_r.at[0])
 
     rows = 2 * HALF
@@ -354,65 +394,78 @@
             hb[z, HALF * k : HALF * (k + 1), 128 * h : 128 * (h + 1)] = res[HALF * h : HALF * (h + 1), :]
         ring_send(hb, g_s, g_r, 0, k)
 
-    ring_step(hb, g_s, g_r, 0)
+    ring_step(hb, g_s, g_r, 0, 0)
+    ring_step(hb, g_s, g_r, 1, 0)
+    ring_step(hb, g_s, g_r, 0, 1)
     weight_last(wob, yo_r, c_r.at[2], KROWS // 2)
-    ring_step(hb, g_s, g_r, 1)
+    ring_step(hb, g_s, g_r, 2, 0)
+    ring_step(hb, g_s, g_r, 1, 1)
     wait_bytes(wob.at[other], c_r.at[2])
+    ring_step(hb, g_s, g_r, 3, 0)
+    ring_step(hb, g_s, g_r, 2, 1)
     acc[...] = jnp.zeros_like(acc)
 
-    def finish(zi):
-        hg = hb[zi]
+    def finish(zi, h):
+        hs = pl.ds(HALF * h, HALF)
+        hg = hb[zi, hs]
         kr = pl.ds(pl.multiple_of(zi % 4 * 256, 256), 256)
         for b in range(4):
-            acc[b] += jnp.dot(hg, wob[zi // 4, b, kr, :], preferred_element_type=F32)
-
-    def near_out(i, _):
-        finish((z + NZ - 2 + i) % NZ)
+            acc[b, hs] += jnp.dot(hg, wob[zi // 4, b, kr, :], preferred_element_type=F32)
+
+    def first_out(i, _):
+        finish(i, 0)
         return 0
 
-    lax.fori_loop(0, 5, near_out, 0)
-    ring_step(hb, g_s, g_r, 2)
-
-    def far_out(i, _):
-        finish((z + 3 + 2 * i) % NZ)
+    def second_out(i, _):
+        finish((z + NZ - 3 + i) % NZ, 1)
         return 0
 
-    lax.fori_loop(0, 2, far_out, 0)
-    ring_step(hb, g_s, g_r, 3)
-    finish((z + 4) % NZ)
+    def reduce_out(h):
+        hs = pl.ds(HALF * h, HALF)
+        for dx in range(1, 4):
+            xt = (x + dx) % NX
+            osb[dx - 1, hs] = acc[xt, hs].astype(BF)
+            go(remote(osb.at[dx - 1, hs], orx.at[dx - 1, hs], o_s.at[h], o_r.at[h], 2 * xt + core, col))
 
     o_copies = []
-    for b in range(4):
-        osb[b] = acc[b].astype(BF)
-        for k in range(2):
-            tr = y if k == 0 else 7 - y
-            ha = core if k == 0 else 1 - core
-            me = jnp.logical_and(tr == row, b == y)
-            src = osb.at[b, pl.ds(HALF * k, HALF)]
-            dst = orx.at[x, ha]
-            rs = o_r.at[2 * x + ha]
-            cp = remote(src, dst, o_s.at[2 * b + k], rs, tr, 8 * b + z)
-            o_copies.append((cp, me))
-
-            @pl.when(me)
-            def _():
-                pltpu.make_async_copy(src, dst, rs).start()
-
-            @pl.when(jnp.logical_not(me))
-            def _():
-                cp.start()
-
+
+    def deliver(h):
+        hs = pl.ds(HALF * h, HALF)
+        wait_bytes(orx.at[:, hs], o_r.at[h])
+        v = acc[x, hs]
+        for i in range(3):
+            v += orx[i, hs].astype(F32)
+        fin[h] = v.astype(BF)
+        tr = y if h == 0 else 7 - y
+        ha = core if h == 0 else 1 - core
+        me = jnp.logical_and(tr == row, x == y)
+        src, dst, rs = fin.at[h], frx.at[ha], f_r.at[ha]
+        cp = remote(src, dst, f_s.at[h], rs, tr, 8 * x + z)
+        o_copies.append((cp, me))
+
+        @pl.when(me)
+        def _():
+            pltpu.make_async_copy(src, dst, rs).start()
+
+        @pl.when(jnp.logical_not(me))
+        def _():
+            cp.start()
+
+    lax.fori_loop(0, NZ, first_out, 0)
+    reduce_out(0)
+    lax.fori_loop(0, 7, second_out, 0)
+    ring_step(hb, g_s, g_r, 3, 1)
+    finish((z + 4) % NZ, 1)
+    reduce_out(1)
+    deliver(0)
+    deliver(1)
     for ha in range(2):
-        for xs in range(4):
-            wait_bytes(orx.at[xs, ha], o_r.at[2 * xs + ha])
-        v = orx[0, ha].astype(F32)
-        for xs in range(1, 4):
-            v += orx[xs, ha].astype(F32)
-        out[HALF * ha : HALF * (ha + 1), :] = v.astype(BF)
+        wait_bytes(frx.at[ha], f_r.at[ha])
+        out[HALF * ha : HALF * (ha + 1), :] = frx[ha]
 
     for cp in sends:
         cp.wait_send()
-    for cp, me in t_copies + o_copies:
+    for cp, me in t_copies + k_copies + o_copies:
 
         @pl.when(jnp.logical_not(me))
         def _():
@@ -452,8 +505,10 @@
         pltpu.VMEM((TOK, 128), F32),
         pltpu.VMEM((2, TOK, 128), BF),
         pltpu.VMEM((NZ, TOK, COLS), BF),
-        pltpu.VMEM((NY, TOK, COLS), BF),
-        pltpu.VMEM((4, 2, HALF, COLS), BF),
+        pltpu.VMEM((3, TOK, COLS), BF),
+        pltpu.VMEM((3, TOK, COLS), BF),
+        pltpu.VMEM((2, HALF, COLS), BF),
+        pltpu.VMEM((2, HALF, COLS), BF),
         dma((2,)), dma((2,)),
         dma((2, 4, 2)), dma((2, 4, 2)),
         dma((2, 4, 2)), dma((2, 4, 2)),
@@ -465,9 +520,10 @@
         dma((1,)), dma((1,)),
         dma((1,)), dma((1,)),
         dma((1,)), dma((1,)),
+        dma((1,)), dma((4,)), dma((4,)), dma((4,)), dma((2, 4)),
         dma((1,)), dma((1,)),
-        dma((1,)), dma((1,)),
-        dma((8,)), dma((8,)),
+        dma((2,)), dma((2,)),
+        dma((2,)), dma((2,)),
     ]
     return pl.pallas_call(
         kernel,

time: 169 us -> 151 us (0.89)
  the two profiles are of different devices: /device:TPU:30 before, /device:TPU:5 now
where the time goes in v2:
time: 151 us
  Pallas kernels  145 us (96%)
  other arithmetic  2.89 us (2%)
  local copies, waits for them, and re-layouts  2.68 us (2%)
    pallas_call x1, Pallas kernels, per_device(): pl.pallas_call(kernel, out_shape=jax.ShapeDtypeStruct((TOK, COLS), BF), i...  145 us

profile of v2, /device:TPU:5, one launch (start us, length us, event | category | flops | bytes accessed | tf_op | source)
XLA Modules:
  0.0 151.1 jit_solution(18325583054227573028)
XLA Ops:
  0.0 1.0 fusion.2
  1.0 0.0 copy-start
  1.0 1.0 pad_maximum_fusion
  2.0 0.0 copy-done
  2.0 0.0 copy-start.1
  2.0 0.2 copy.7
  2.2 0.7 copy-done.1
  2.9 0.2 copy.8
  3.0 0.1 fusion
  3.1 0.8 fusion.1.wkv
  3.9 145.5 %shard_map.64 = bf16[512,256]{1,0:T(8,128)(2,1)} custom-call(bf16[512,256]{1,0:T(8,128)(2,1)} %hid.1, f32[1,8192]{1,0:T(1,128)} %bitcast.1, bf16[1024,256]{1,0:T(8,128)(2,1)} %wq.1, bf16[512,128]{1,0:T(8,128)(2,1)} %fusion.1.wkv, bf16[1024,256]{1,0:T(8,128)(2,1)} %wo.1, f32[512,128]{1,0:T(8,128)} %get-tuple-element.8.ctab, f32[512,128]{1,0:T(8,128)} %get-tuple-element.9.stab), custom_call_target="tpu_custom_call" | custom-call | tf_op jit(solution)/shard_map/pallas_call | solution.py:528
  149.4 1.7 %copy.10 = bf16[512,256]{1,0:T(8,128)(2,1)} copy(bf16[512,256]{1,0:T(8,128)(2,1)} %shard_map.64) | data formatting | bytes 524288
  (2 shorter events, 0.0 us)
Async XLA Ops:
  1.0 1.0 copy-start
  2.0 0.8 copy-start.1

commit v3 on v2

--- a/solution.py
+++ b/solution.py
@@ -190,13 +190,7 @@
     wait_bytes(kvw.at[core, bot, l2], yk_r.at[1, 1])
     go(remote(kvw.at[core, :, l2], kvw.at[core, :, l2], c_s.at[0], c_r.at[1], prow, col))
 
-    go(remote(wo, wob.at[core, y], yo_s.at[0, 0], yo_r.at[0, 0], row, yr))
-    go(remote(wo, wob.at[core, y], yo_s.at[1, 0], yo_r.at[1, 0], row, yl))
-    go(remote(wo, wob.at[core, y], c_s.at[0], c_r.at[2], prow, col))
-
     other = 1 - core
-    ring_step(hbuf, z_s, z_r, 3, 0)
-    ring_step(hbuf, z_s, z_r, 2, 1)
     wait_bytes(wbuf.at[other], c_r.at[0])
     wait_bytes(kvw.at[other], c_r.at[1])
     for c in own:
@@ -251,17 +245,20 @@
             go(remote(qs.at[dx - 1, hs], qrx.at[dx - 1, hs], q_s.at[0], q_r.at[0], 2 * xt + core, col))
 
     def first_half(i, _):
-        project(i, 0)
+        project((z + NZ - 3 + i) % NZ, 0)
         return 0
 
     def second_half(i, _):
         project((z + NZ - 3 + i) % NZ, 1)
         return 0
 
-    lax.fori_loop(0, NZ, first_half, 0)
+    lax.fori_loop(0, 3, first_half, 0)
+    ring_step(hbuf, z_s, z_r, 3, 0)
+    lax.fori_loop(3, 5, first_half, 0)
+    ring_step(hbuf, z_s, z_r, 2, 1)
+    lax.fori_loop(5, NZ, first_half, 0)
     reduce_kv(0)
     reduce_q(0)
-    weight_hop(wob, yo_s, yo_r, c_r.at[2], KROWS // 2)
     lax.fori_loop(0, 7, second_half, 0)
     ring_step(hbuf, z_s, z_r, 3, 1)
     project((z + 4) % NZ, 1)
@@ -355,6 +352,10 @@
         to_partner(far)
     wait_bytes(kvb.at[pl.ds(0, 16)], p_r.at[0])
 
+    go(remote(wo, wob.at[core, y], yo_s.at[0, 0], yo_r.at[0, 0], row, yr))
+    go(remote(wo, wob.at[core, y], yo_s.at[1, 0], yo_r.at[1, 0], row, yl))
+    go(remote(wo, wob.at[core, y], c_s.at[0], c_r.at[2], prow, col))
+
     rows = 2 * HALF
     tri = (
         lax.broadcasted_iota(jnp.int32, (rows, HALF), 0) % HALF
@@ -395,14 +396,13 @@
         ring_send(hb, g_s, g_r, 0, k)
 
     ring_step(hb, g_s, g_r, 0, 0)
+    weight_hop(wob, yo_s, yo_r, c_r.at[2], KROWS // 2)
     ring_step(hb, g_s, g_r, 1, 0)
     ring_step(hb, g_s, g_r, 0, 1)
-    weight_last(wob, yo_r, c_r.at[2], KROWS // 2)
     ring_step(hb, g_s, g_r, 2, 0)
     ring_step(hb, g_s, g_r, 1, 1)
+    weight_last(wob, yo_r, c_r.at[2], KROWS // 2)
     wait_bytes(wob.at[other], c_r.at[2])
-    ring_step(hb, g_s, g_r, 3, 0)
-    ring_step(hb, g_s, g_r, 2, 1)
     acc[...] = jnp.zeros_like(acc)
 
     def finish(zi, h):
@@ -413,7 +413,7 @@
             acc[b, hs] += jnp.dot(hg, wob[zi // 4, b, kr, :], preferred_element_type=F32)
 
     def first_out(i, _):
-        finish(i, 0)
+        finish((z + NZ - 3 + i) % NZ, 0)
         return 0
 
     def second_out(i, _):
@@ -451,7 +451,11 @@
         def _():
             cp.start()
 
-    lax.fori_loop(0, NZ, first_out, 0)
+    lax.fori_loop(0, 3, first_out, 0)
+    ring_step(hb, g_s, g_r, 3, 0)
+    lax.fori_loop(3, 5, first_out, 0)
+    ring_step(hb, g_s, g_r, 2, 1)
+    lax.fori_loop(5, NZ, first_out, 0)
     reduce_out(0)
     lax.fori_loop(0, 7, second_out, 0)
     ring_step(hb, g_s, g_r, 3, 1)

time: 151 us -> 143 us (0.947)
  Pallas kernels: 145 us -> 137 us
    pallas_call x1, Pallas kernels: 145 us -> 137 us  [per_device(): pl.pallas_call(kernel, out_shape=jax.ShapeDtypeStruct((TOK, COLS), BF), i...]
where the time goes in v3:
time: 143 us
  Pallas kernels  137 us (96%)
  other arithmetic  2.89 us (2%)
  local copies, waits for them, and re-layouts  2.68 us (2%)
    pallas_call x1, Pallas kernels, per_device(): pl.pallas_call(kernel, out_shape=jax.ShapeDtypeStruct((TOK, COLS), BF), i...  137 us

profile of v3, /device:TPU:5, one launch (start us, length us, event | category | flops | bytes accessed | tf_op | source)
XLA Modules:
  0.0 142.7 jit_solution(6442192990695556535)
XLA Ops:
  0.0 1.0 fusion.2
  1.0 0.0 copy-start
  1.0 1.0 pad_maximum_fusion
  2.0 0.0 copy-done
  2.0 0.0 copy-start.1
  2.0 0.2 copy.7
  2.2 0.7 copy-done.1
  2.9 0.2 copy.8
  3.0 0.1 fusion
  3.1 0.8 fusion.1.wkv
  3.9 137.1 %shard_map.64 = bf16[512,256]{1,0:T(8,128)(2,1)} custom-call(bf16[512,256]{1,0:T(8,128)(2,1)} %hid.1, f32[1,8192]{1,0:T(1,128)} %bitcast.1, bf16[1024,256]{1,0:T(8,128)(2,1)} %wq.1, bf16[512,128]{1,0:T(8,128)(2,1)} %fusion.1.wkv, bf16[1024,256]{1,0:T(8,128)(2,1)} %wo.1, f32[512,128]{1,0:T(8,128)} %get-tuple-element.8.ctab, f32[512,128]{1,0:T(8,128)} %get-tuple-element.9.stab), custom_call_target="tpu_custom_call" | custom-call | tf_op jit(solution)/shard_map/pallas_call | solution.py:532
  141.0 1.7 %copy.10 = bf16[512,256]{1,0:T(8,128)(2,1)} copy(bf16[512,256]{1,0:T(8,128)(2,1)} %shard_map.64) | data formatting | bytes 524288
  (2 shorter events, 0.0 us)
Async XLA Ops:
  1.0 1.0 copy-start
  2.0 0.8 copy-start.1

commit v4 on v3

--- a/solution.py
+++ b/solution.py
@@ -25,8 +25,8 @@
 
 
 def kernel(
-    hid, gain, wq, wkv, wo, ctab, stab, out,
-    hbuf, wbuf, kvw, wob, acc, kvacc, ssacc, qs, qrx, kvs, kvrx, kvb, ssb, rcol, qb, hb, osb, orx, fin, frx,
+    hid, gain, freq, wq, wkv, wo, out,
+    ctab, stab, hbuf, wbuf, kvw, wob, acc, kvacc, ssacc, qs, qrx, kvs, kvrx, kvb, ssb, rcol, qb, hb, osb, orx, fin, frx,
     t_s, t_r, z_s, z_r, g_s, g_r, y_s, y_r, yk_s, yk_r, yo_s, yo_r,
     c_s, c_r, loc, q_s, q_r, ss_s, ss_r, k_s, k_r, b_s, b_r, bl_r, br_r, bf_r, p_s, p_r, o_s, o_r, f_s, f_r,
 ):
@@ -147,6 +147,13 @@
     for h in range(2):
         wait_bytes(hbuf.at[z, pl.ds(HALF * h, HALF)], t_r.at[h])
         ring_send(hbuf, z_s, z_r, 0, h)
+
+    spot = lax.broadcasted_iota(jnp.int32, (TOK, HD), 0)
+    spot = jnp.where(spot < HALF, HALF * d + spot, HALF * (14 - d) + spot)
+    angle = spot.astype(F32) * freq[...]
+    ctab[...] = jnp.cos(angle)
+    sine = jnp.sin(angle)
+    stab[...] = jnp.where(lax.broadcasted_iota(jnp.int32, (TOK, HD), 1) < HD // 2, -sine, sine)
 
     ring_step(hbuf, z_s, z_r, 0, 0)
 
@@ -395,6 +402,7 @@
             hb[z, HALF * k : HALF * (k + 1), 128 * h : 128 * (h + 1)] = res[HALF * h : HALF * (h + 1), :]
         ring_send(hb, g_s, g_r, 0, k)
 
+    acc[...] = jnp.zeros_like(acc)
     ring_step(hb, g_s, g_r, 0, 0)
     weight_hop(wob, yo_s, yo_r, c_r.at[2], KROWS // 2)
     ring_step(hb, g_s, g_r, 1, 0)
@@ -403,7 +411,6 @@
     ring_step(hb, g_s, g_r, 1, 1)
     weight_last(wob, yo_r, c_r.at[2], KROWS // 2)
     wait_bytes(wob.at[other], c_r.at[2])
-    acc[...] = jnp.zeros_like(acc)
 
     def finish(zi, h):
         hs = pl.ds(HALF * h, HALF)
@@ -477,22 +484,17 @@
 
 
 def per_device(hidden, norm_gain, wq, wk, wv, wo):
-    row, col = lax.axis_index("row"), lax.axis_index("col")
-    d = 2 * (col // NZ) + row % 2
-    i = jnp.arange(TOK)
-    positions = jnp.where(i < HALF, HALF * d + i, HALF * (15 - d) + i - HALF)
     steps = jnp.arange(HD // 2).astype(F32)
     freqs = 10000.0 ** (-steps / (HD // 2))
-    angles = positions.astype(F32)[:, None] * freqs[None, :]
-    cosine, sine = jnp.cos(angles), jnp.sin(angles)
-    ctab = jnp.concatenate([cosine, cosine], axis=1)
-    stab = jnp.concatenate([-sine, sine], axis=1)
+    freq = jnp.concatenate([freqs, freqs]).reshape(1, HD)
     both = jnp.concatenate([wk, wv], axis=1)
     wkv = jnp.concatenate([both[:512], both[512:]], axis=1)
     dma = pltpu.SemaphoreType.DMA
     vmem = pl.BlockSpec(memory_space=pltpu.VMEM)
     anyw = pl.BlockSpec(memory_space=pl.ANY)
     scratch = [
+        pltpu.VMEM((TOK, HD), F32),
+        pltpu.VMEM((TOK, HD), F32),
         pltpu.VMEM((NZ, TOK, COLS), BF),
         pltpu.VMEM((2, NY, KROWS, COLS), BF),
         pltpu.VMEM((2, 512, 512), BF),
@@ -532,13 +534,13 @@
     return pl.pallas_call(
         kernel,
         out_shape=jax.ShapeDtypeStruct((TOK, COLS), BF),
-        in_specs=[anyw, vmem, anyw, anyw, anyw, vmem, vmem],
+        in_specs=[anyw, vmem, vmem, anyw, anyw, anyw],
         out_specs=vmem,
         scratch_shapes=scratch,
         compiler_params=pltpu.CompilerParams(
             collective_id=0, has_side_effects=True, vmem_limit_bytes=56 * 1024 * 1024
         ),
-    )(hidden, norm_gain.reshape(1, D), wq, wkv, wo, ctab, stab)
+    )(hidden, norm_gain.reshape(1, D), freq, wq, wkv, wo)
 
 
 def solution(mesh):

time: 143 us -> 141 us (0.986)
    unnamed x7 -> x5, local copies, waits for them, and re-layouts: 2.68 us -> 2.88 us
where the time goes in v4:
time: 141 us
  Pallas kernels  137 us (97%)
  local copies, waits for them, and re-layouts  2.88 us (2%)
  other arithmetic  1.53 us (1%)
    pallas_call x1, Pallas kernels, per_device(): pl.pallas_call(kernel, out_shape=jax.ShapeDtypeStruct((TOK, COLS), BF), i...  137 us
    unnamed x5, local copies, waits for them, and re-layouts  2.88 us

profile of v4, /device:TPU:5, one launch (start us, length us, event | category | flops | bytes accessed | tf_op | source)
XLA Modules:
  0.0 141.3 jit_solution(3406341622980010339)
XLA Ops:
  0.0 0.0 copy-start
  0.0 1.0 copy.7
  1.0 0.0 copy-done
  1.1 0.2 copy.8
  1.2 0.1 fusion
  1.4 0.8 fusion.1.wkv
  2.2 0.6 maximum_bitcast_fusion.freq
  2.8 136.8 %shard_map.64 = bf16[512,256]{1,0:T(8,128)(2,1)} custom-call(bf16[512,256]{1,0:T(8,128)(2,1)} %hid.1, f32[1,8192]{1,0:T(1,128)} %bitcast.3, f32[1,128]{1,0:T(1,128)} %maximum_bitcast_fusion.freq, bf16[1024,256]{1,0:T(8,128)(2,1)} %wq.1, bf16[512,128]{1,0:T(8,128)(2,1)} %fusion.1.wkv, bf16[1024,256]{1,0:T(8,128)(2,1)} %wo.1), custom_call_target="tpu_custom_call" | custom-call | tf_op jit(solution)/shard_map/pallas_call | solution.py:534
  139.6 1.7 %copy.10 = bf16[512,256]{1,0:T(8,128)(2,1)} copy(bf16[512,256]{1,0:T(8,128)(2,1)} %shard_map.64) | data formatting | bytes 524288
  (1 shorter events, 0.0 us)
Async XLA Ops:
  0.0 1.0 copy-start
